TPU v7x, 32 devices: a whole 2x2x4 slice. The times are simulated.
32 devices in a mesh: edata: 4 (over z), expert: 8 (over y, x, core).
Axes of the slice: x: 2, y: 2, z: 4, core: 2. Of those that a mesh axis runs over, the one named last changes fastest.
Arguments:
- tokens: bfloat16 [1024, 4096], P('expert', 'edata'), may hold values from -6 to 6
- grad_out: bfloat16 [1024, 4096], P('expert', 'edata'), may hold values from -6 to 6
- expert_ids: int32 [1024, 8], P('expert'), may hold values from 0 to 15, all different within a row; in each aligned block of 128 rows (0 to 127, 128 to 255, ...) at most 80 rows name the same one
- route_prob: float32 [1024, 8], P('expert'), may hold values from 0.05 to 0.5
- w_gate: bfloat16 [16, 1024, 4096], P('expert', 'edata'), may hold values from -0.09375 to 0.09375
- w_up: bfloat16 [16, 1024, 4096], P('expert', 'edata'), may hold values from -0.09375 to 0.09375
- w_down: bfloat16 [16, 1024, 4096], P('expert', 'edata'), may hold values from -0.1875 to 0.1875
Outputs:
- grad_tokens: bfloat16 [1024, 4096], P('expert', 'edata')
- grad_gate: bfloat16 [16, 1024, 4096], P('expert', 'edata')
- grad_up: bfloat16 [16, 1024, 4096], P('expert', 'edata')
- grad_down: bfloat16 [16, 1024, 4096], P('expert', 'edata')
Inputs may be any that keep to these rules, and one draw needn't show every extreme that they name: `expert_ids`: each token names 8 different experts. Among the tokens of one aligned block of 128 no expert is named more than 80 times, and in every draw some expert is named exactly 80 times in some block.
All inputs are finite; a program needn't handle non-finite values.
Results may differ from a plain program's by a relative error of at most 0.012.
Values may be sent and summed in bfloat16 or wider, within the bound.
A program may use at most 192 MiB of HBM per device.

v0:
```python
import jax
import jax.numpy as jnp
from jax import lax
from jax.sharding import PartitionSpec as P


def ranks(onehot):
    pair_count = onehot.shape[-2]
    row = lax.broadcasted_iota(jnp.int32, (pair_count, pair_count), 0)
    col = lax.broadcasted_iota(jnp.int32, (pair_count, pair_count), 1)
    tri = (col < row).astype(jnp.bfloat16)
    earlier = jnp.einsum(
        "pq,...qe->...pe", tri, onehot.astype(jnp.bfloat16), preferred_element_type=jnp.float32
    )
    return earlier.astype(jnp.int32)


def body(tokens, grad_out, expert_ids, route_prob, w_gate, w_up, w_down):
    token_count, top_count = expert_ids.shape
    local_experts = w_gate.shape[0]
    expert_devices = lax.axis_size("expert")
    me = lax.axis_index("expert")
    experts_all = expert_devices * local_experts
    capacity = token_count * top_count * 5 // (4 * experts_all)
    pair_count = token_count * top_count
    cap_iota = jnp.arange(capacity, dtype=jnp.int32)
    routing = jnp.stack([expert_ids.astype(jnp.float32), route_prob])
    routing = lax.all_gather(routing, "expert", axis=1, tiled=False)
    all_ids, all_prob = (routing[0].astype(jnp.int32), routing[1])
    mine = me * local_experts + jnp.arange(local_experts, dtype=jnp.int32)
    named = all_ids.reshape(expert_devices, pair_count)[:, :, None] == mine
    rank = ranks(named)
    hit = named[..., None] & (rank[..., None] == cap_iota)
    hit = hit.reshape(expert_devices, token_count, top_count, local_experts, capacity)
    pick = jnp.sum(hit.astype(jnp.int32), 2).astype(jnp.bfloat16)
    prob_of = jnp.sum(jnp.where(hit, all_prob[:, :, :, None, None], 0.0), (1, 2))
    both = lax.all_gather(jnp.stack([tokens, grad_out]), "edata", axis=2, tiled=True)
    both = lax.all_gather(both, "expert", axis=1, tiled=False)
    all_x, all_dy = (both[0], both[1])
    slot_x = jnp.einsum("stxc,std->sxcd", pick, all_x, preferred_element_type=jnp.float32).astype(
        jnp.bfloat16
    )
    slot_dy = jnp.einsum("stxc,std->sxcd", pick, all_dy, preferred_element_type=jnp.float32)
    slot_dy = (prob_of[..., None] * slot_dy).astype(jnp.bfloat16)
    gate_value = jnp.einsum("sxcd,xfd->sxcf", slot_x, w_gate, preferred_element_type=jnp.float32)
    up_value = jnp.einsum("sxcd,xfd->sxcf", slot_x, w_up, preferred_element_type=jnp.float32)
    sigma = jax.nn.sigmoid(gate_value)
    active = gate_value * sigma
    hidden = (active * up_value).astype(jnp.bfloat16)
    back = jnp.einsum("sxcd,xfd->sxcf", slot_dy, w_down, preferred_element_type=jnp.float32)
    gate_grad = (back * up_value * sigma * (1.0 + gate_value * (1.0 - sigma))).astype(jnp.bfloat16)
    up_grad = (back * active).astype(jnp.bfloat16)
    grad_gate = jnp.einsum(
        "sxcf,sxcd->xfd", gate_grad, slot_x, preferred_element_type=jnp.float32
    ).astype(jnp.bfloat16)
    grad_up = jnp.einsum(
        "sxcf,sxcd->xfd", up_grad, slot_x, preferred_element_type=jnp.float32
    ).astype(jnp.bfloat16)
    grad_down = jnp.einsum(
        "sxcf,sxcd->xfd", hidden, slot_dy, preferred_element_type=jnp.float32
    ).astype(jnp.bfloat16)
    partial_value = jnp.einsum(
        "sxcf,xfd->sxcd", gate_grad, w_gate, preferred_element_type=jnp.float32
    )
    partial_value = partial_value + jnp.einsum(
        "sxcf,xfd->sxcd", up_grad, w_up, preferred_element_type=jnp.float32
    )
    partial_value = partial_value.astype(jnp.bfloat16)
    returned = lax.all_to_all(
        partial_value.reshape(expert_devices, local_experts * capacity, -1),
        "expert",
        split_axis=0,
        concat_axis=0,
        tiled=True,
    )
    width = returned.shape[-1]
    own = expert_ids.reshape(pair_count, 1) == jnp.arange(experts_all, dtype=jnp.int32)
    slot = jnp.sum(jnp.where(own, ranks(own), 0), 1)
    back_hit = own[:, :, None] & (slot[:, None, None] == cap_iota)
    gather_back = jnp.sum(
        back_hit.reshape(token_count, top_count, experts_all * capacity).astype(jnp.int32), 1
    ).astype(jnp.bfloat16)
    per_token = jnp.einsum(
        "tq,qd->td",
        gather_back,
        returned.reshape(experts_all * capacity, width),
        preferred_element_type=jnp.float32,
    )
    grad_tokens = lax.psum_scatter(per_token, "edata", scatter_dimension=1, tiled=True).astype(
        jnp.bfloat16
    )
    return (grad_tokens, grad_gate, grad_up, grad_down)


def solution(mesh):
    placed = (
        P("expert", "edata"),
        P("expert", "edata"),
        P("expert", None),
        P("expert", None),
        P("expert", "edata", None),
        P("expert", "edata", None),
        P("expert", "edata", None),
    )
    return jax.shard_map(
        body,
        mesh=mesh,
        in_specs=placed,
        out_specs=(
            P("expert", "edata"),
            P("expert", "edata", None),
            P("expert", "edata", None),
            P("expert", "edata", None),
        ),
        check_vma=False,
    )
```

profile of v0, /device:TPU:0, one launch (start us, length us, event | category | flops | bytes accessed | tf_op | source)
XLA Modules:
  0.0 408.3 jit_solution(9152429621475397026)
XLA Ops:
  7.2 1.9 pad_maximum_fusion
  9.2 49.4 %all-gather.5.cloned.1.call-done = bf16[2,128,4096]{2,1,0:T(8,128)(2,1)} async-done(((bf16[2,128,1024]{2,1,0:T(8,128)(2,1)}), bf16[2,128,4096]{2,1,0:T(8,128)(2,1)}) %all-gather.5.cloned.1.call-update) | async-done | bytes 2097168 | tf_op jit(solution)/shard_map/all_gather | solution.py:37
  59.9 9.0 %all-gather = f32[2,1024,8]{1,2,0:T(8,128)S(1)} all-gather(f32[2,128,8]{1,2,0:T(8,128)S(1)} %pad_maximum_fusion.1), channel_id=2, replica_groups=mesh['edata'=4,'expert'=8] {'expert'}, dimensions={1}, use_global_device_ids=true | all-gather | bytes 73728 | tf_op jit(solution)/shard_map/all_gather | solution.py:28
  73.7 75.3 %all-gather.7.cloned.1.call-done = bf16[2,1024,4096]{2,1,0:T(8,128)(2,1)} async-done(((bf16[2,128,4096]{2,1,0:T(8,128)(2,1)}), bf16[2,1024,4096]{2,1,0:T(8,128)(2,1)}) %all-gather.7.cloned.1.call-update) | async-done | bytes 16777232 | tf_op jit(solution)/shard_map/all_gather | solution.py:38
  149.0 9.5 %fusion.65 = (bf16[1,1024,4096]{2,1,0:T(8,128)(2,1)}, bf16[1,1024,4096]{2,1,0:T(8,128)(2,1)S(1)}) fusion(bf16[2,1024,4096]{2,1,0:T(8,128)(2,1)} %all-gather.7.cloned.1.call-done), kind=kLoop, calls=%fused_computation.65 | loop fusion | bytes 33554432 | tf_op jit(solution)/shard_map/slice | solution.py:39
  158.5 5.5 %convolution_convert_fusion = bf16[8,2,80,4096]{3,2,1,0:T(8,128)(2,1)} fusion(bf16[8,128,4096,1]{2,1,3,0:T(8,128)(2,1)S(1)} %bitcast.84, s32[8,128,2,80]{1,3,2,0:T(8,128)S(1)} %convert_reduce_fusion), kind=kOutput, calls=%fused_computation.11 | convolution fusion | flops 1347584000 | bytes 19529728 | tf_op jit(solution)/shard_map/stxc,std->sxcd/dot_general | solution.py:40
  163.9 9.3 %fusion.35 = f32[8,2,80,256]{3,2,0,1:T(8,128)} fusion(bf16[2,256,4096]{2,1,0:T(8,128)(2,1)} %param.11, bf16[8,2,80,4096]{3,2,1,0:T(8,128)(2,1)} %convolution_convert_fusion), kind=kOutput, calls=%fused_computation.35 | convolution fusion | flops 2684354560 | bytes 15990784 | tf_op jit(solution)/shard_map/sxcd,xfd->sxcf/dot_general | solution.py:45
  173.2 9.3 %fusion.30 = f32[8,2,80,256]{3,2,0,1:T(8,128)} fusion(bf16[2,256,4096]{2,1,0:T(8,128)(2,1)} %param.12, bf16[8,2,80,4096]{3,2,1,0:T(8,128)(2,1)} %convolution_convert_fusion), kind=kOutput, calls=%fused_computation.34 | convolution fusion | flops 2684354560 | bytes 15990784 | tf_op jit(solution)/shard_map/sxcd,xfd->sxcf/dot_general | solution.py:46
  182.5 5.4 %multiply_convert_fusion = bf16[8,2,80,4096]{3,2,1,0:T(8,128)(2,1)} fusion(f32[8,2,80]{2,1,0:T(2,128)S(1)} %select_reduce_fusion, bf16[8,128,4096,1]{2,1,3,0:T(8,128)(2,1)S(1)} %bitcast.87, s32[8,128,2,80]{1,3,2,0:T(8,128)S(1)} %convert_reduce_fusion), kind=kOutput, calls=%fused_computation.1 | convolution fusion | flops 1352826880 | bytes 19534848 | tf_op jit(solution)/shard_map/stxc,std->sxcd/dot_general | solution.py:43
  187.9 9.4 %multiply_convert_fusion.2 = (bf16[8,2,80,256]{3,2,0,1:T(8,128)(2,1)S(1)}, bf16[8,2,80,256]{3,2,0,1:T(8,128)(2,1)S(1)}) fusion(f32[8,2,80,256]{3,2,0,1:T(8,128)} %fusion.35, f32[8,2,80,256]{3,2,0,1:T(8,128)} %fusion.30, bf16[2,256,4096]{2,1,0:T(8,128)(2,1)} %param.13, bf16[8,2,80,4096]{3,2,1,0:T(8,128)(2,1)} %multiply_convert_fusion), kind=kOutput, calls=%fused_computation.38 | convolution fusion | flops 2688614400 | bytes 18612224 | tf_op jit(solution)/shard_map/sxcd,xfd->sxcf/dot_general | solution.py:50
  197.3 8.7 %fusion.20 = f32[2,8,80,4096]{3,2,1,0:T(8,128)} fusion(bf16[8,2,80,256]{3,2,0,1:T(8,128)(2,1)S(1)} %get-tuple-element.7, bf16[2,256,4096]{2,1,0:T(8,128)(2,1)S(1)} %copy-done), kind=kOutput, calls=%fused_computation.24 | convolution fusion | flops 2684354560 | bytes 25821184 | tf_op jit(solution)/shard_map/sxcf,xfd->sxcd/dot_general | solution.py:62
  206.0 13.0 %fusion = bf16[8,2,80,4096]{3,2,0,1:T(8,128)(2,1)} fusion(f32[2,8,80,4096]{3,2,1,0:T(8,128)} %fusion.20, bf16[8,2,80,256]{3,2,0,1:T(8,128)(2,1)S(1)} %get-tuple-element.6, bf16[2,256,4096]{2,1,0:T(8,128)(2,1)} %param.12), kind=kOutput, calls=%fused_computation.2 | convolution fusion | flops 2694840320 | bytes 36306944 | tf_op jit(solution)/shard_map/sxcf,xfd->sxcd/dot_general | solution.py:65
  219.0 9.4 %copy.42 = bf16[8,2,80,4096]{3,2,1,0:T(8,128)(2,1)} copy(bf16[8,2,80,4096]{3,2,0,1:T(8,128)(2,1)} %fusion) | data formatting | bytes 20971520 | tf_op jit(solution)/shard_map/convert_element_type | solution.py:68
  228.4 5.3 %all-to-all-start = ((bf16[8,160,4096]{2,1,0:T(8,128)(2,1)}), bf16[8,160,4096]{2,1,0:T(8,128)(2,1)}, u32[]{:S(2)}, u32[]{:S(2)}) async-start(bf16[8,160,4096]{2,1,0:T(8,128)(2,1)} %bitcast.83), calls=%async_computation | async-start | bytes 20971520 | tf_op jit(solution)/shard_map/all_to_all | solution.py:69
  235.0 7.9 %and_convert_fusion = s32[1024,16,80]{2,1,0:T(8,128)} fusion(pred[1024,80]{1,0:T(8,128)(4,1)S(1)} %iota_compare_fusion.9, pred[1024,16]{1,0:T(8,128)(4,1)S(1)} %copy.35), kind=kLoop, calls=%fused_computation.10 | loop fusion | flops 2621440 | bytes 5341184 | tf_op jit(solution)/shard_map/convert_element_type | solution.py:81
  242.8 9.1 %reshape.90 = s32[128,8,1280]{2,1,0:T(8,128)} reshape(s32[1024,16,80]{2,1,0:T(8,128)} %and_convert_fusion) | data formatting | bytes 10485760 | tf_op jit(solution)/shard_map/convert_element_type | solution.py:81
  251.9 3.7 reduce_sum.37
  255.7 94.6 %all-to-all-done = bf16[8,160,4096]{2,1,0:T(8,128)(2,1)} async-done(((bf16[8,160,4096]{2,1,0:T(8,128)(2,1)}), bf16[8,160,4096]{2,1,0:T(8,128)(2,1)}, u32[]{:S(2)}, u32[]{:S(2)}) %all-to-all-start) | async-done | bytes 10485792 | tf_op jit(solution)/shard_map/all_to_all | solution.py:69
  350.2 6.8 %fusion.55 = f32[128,4096]{1,0:T(8,128)} fusion(bf16[1280,4096]{1,0:T(8,128)(2,1)} %bitcast.26, s32[128,1280]{1,0:T(8,128)S(1)} %reduce_sum.37), kind=kOutput, calls=%fused_computation.49 | convolution fusion | flops 1342341120 | bytes 13238272 | tf_op jit(solution)/shard_map/tq,qd->td/dot_general | solution.py:83
  357.1 9.2 %bitcast_convert_fusion.1 = bf16[2,256,4096]{2,1,0:T(8,128)(2,1)} fusion(bf16[8,2,80,256]{3,2,0,1:T(8,128)(2,1)S(1)} %get-tuple-element.6, bf16[8,2,80,4096]{3,2,1,0:T(8,128)(2,1)} %convolution_convert_fusion), kind=kOutput, calls=%fused_computation.8 | convolution fusion | flops 2686451712 | bytes 15335424 | tf_op jit(solution)/shard_map/sxcf,sxcd->xfd/dot_general | solution.py:56
  366.3 9.3 %bitcast_convert_fusion.2 = bf16[2,256,4096]{2,1,0:T(8,128)(2,1)} fusion(bf16[8,2,80,256]{3,2,0,1:T(8,128)(2,1)S(1)} %get-tuple-element.7, bf16[8,2,80,4096]{3,2,1,0:T(8,128)(2,1)} %convolution_convert_fusion), kind=kOutput, calls=%fused_computation.9 | convolution fusion | flops 2686451712 | bytes 15335424 | tf_op jit(solution)/shard_map/sxcf,sxcd->xfd/dot_general | solution.py:53
  375.6 5.3 %bitcast_convert_fusion = bf16[2,256,4096]{2,1,0:T(8,128)(2,1)} fusion(bf16[8,2,80,4096]{3,2,1,0:T(8,128)(2,1)S(1)} %bitcast.89, f32[8,2,80,256]{3,2,0,1:T(8,128)S(1)} %copy-done.3, f32[8,2,80,256]{3,2,0,1:T(8,128)S(1)} %copy-done.2), kind=kOutput, calls=%fused_computation.7 | convolution fusion | flops 2688417792 | bytes 17301504 | tf_op jit(solution)/shard_map/sxcf,sxcd->xfd/dot_general | solution.py:59
  381.0 19.0 %reduce-scatter.2.cloned.1.call-done = f32[128,1024]{1,0:T(8,128)} async-done(((f32[128,4096]{1,0:T(8,128)}), f32[128,1024]{1,0:T(8,128)}) %reduce-scatter.2.cloned.1.call-update) | async-done | bytes 524304 | tf_op jit(solution)/shard_map/reduce_scatter | solution.py:89
  400.0 1.8 convert_element_type.96
  (45 shorter events, 7.4 us)
Async XLA Ops:
  7.2 51.4 %all-gather.5.cloned.1.call-start = ((), (), s32[]{:S(2)}) async-start(), calls=%async_computation.2 | async-start | bytes 2621440 | tf_op jit(solution)/shard_map/all_gather | solution.py:37
  9.1 139.9 %all-gather.7.cloned.1.call-start = ((), (), s32[]{:S(2)}) async-start(), calls=%async_computation.4 | async-start | bytes 18874368 | tf_op jit(solution)/shard_map/all_gather | solution.py:38
  163.9 18.6 %slice-start = ((s8[8388608]{0:T(1024)(128)(4,1)}), s8[4194304]{0:T(1024)(128)(4,1)S(1)}, s32[]{:S(2)}) async-start(s8[8388608]{0:T(1024)(128)(4,1)} %bitcast.85), calls=%async_computation.5 | async-start | bytes 8388608
  173.2 9.3 %slice-start.1 = ((s8[8388608]{0:T(1024)(128)(4,1)}), s8[4194304]{0:T(1024)(128)(4,1)S(1)}, s32[]{:S(2)}) async-start(s8[8388608]{0:T(1024)(128)(4,1)} %bitcast.85), calls=%async_computation.6 | async-start | bytes 8388608
  187.9 9.4 %copy-start = (bf16[2,256,4096]{2,1,0:T(8,128)(2,1)S(1)}, bf16[2,256,4096]{2,1,0:T(8,128)(2,1)}, u32[]{:S(2)}) copy-start(bf16[2,256,4096]{2,1,0:T(8,128)(2,1)} %param.11) | copy-start | bytes 12582916
  228.4 5.4 %copy-start.1 = (s32[128,8]{0,1:T(8,128)S(1)}, s32[128,8]{0,1:T(8,128)}, u32[]{:S(2)}) copy-start(s32[128,8]{0,1:T(8,128)} %param.9) | copy-start | bytes 12292
  228.4 121.8 %all-to-all-start = ((bf16[8,160,4096]{2,1,0:T(8,128)(2,1)}), bf16[8,160,4096]{2,1,0:T(8,128)(2,1)}, u32[]{:S(2)}, u32[]{:S(2)}) async-start(bf16[8,160,4096]{2,1,0:T(8,128)(2,1)} %bitcast.83), calls=%async_computation | async-start | bytes 20971520 | tf_op jit(solution)/shard_map/all_to_all | solution.py:69
  233.7 166.3 %reduce-scatter.2.cloned.1.call-start = ((), (), s32[]{:S(2)}) async-start(), calls=%async_computation.3 | async-start | bytes 2621440 | tf_op jit(solution)/shard_map/reduce_scatter | solution.py:89
  357.1 18.5 %slice-start.2 = ((s8[10485760]{0:T(1024)(128)(4,1)}), s8[4194304]{0:T(1024)(128)(4,1)S(1)}, s32[]{:S(2)}) async-start(s8[10485760]{0:T(1024)(128)(4,1)} %bitcast.88), calls=%async_computation.7 | async-start | bytes 8388608
  357.1 18.5 %slice-start.3 = ((s8[10485760]{0:T(1024)(128)(4,1)}), s8[4194304]{0:T(1024)(128)(4,1)S(1)}, s32[]{:S(2)}) async-start(s8[10485760]{0:T(1024)(128)(4,1)} %bitcast.88), calls=%async_computation.8 | async-start | bytes 8388608
  366.3 9.3 %slice-start.4 = ((s8[10485760]{0:T(1024)(128)(4,1)}), s8[2097152]{0:T(1024)(128)(4,1)S(1)}, s32[]{:S(2)}) async-start(s8[10485760]{0:T(1024)(128)(4,1)} %bitcast.88), calls=%async_computation.9 | async-start | bytes 4194304
  366.3 9.3 %copy-start.2 = (f32[8,2,80,256]{3,2,0,1:T(8,128)S(1)}, f32[8,2,80,256]{3,2,0,1:T(8,128)}, u32[]{:S(2)}) copy-start(f32[8,2,80,256]{3,2,0,1:T(8,128)} %fusion.35) | copy-start | bytes 3932164
  366.3 9.3 %copy-start.3 = (f32[8,2,80,256]{3,2,0,1:T(8,128)S(1)}, f32[8,2,80,256]{3,2,0,1:T(8,128)}, u32[]{:S(2)}) copy-start(f32[8,2,80,256]{3,2,0,1:T(8,128)} %fusion.30) | copy-start | bytes 3932164
Sparse Core Ops, SparseCore 0:
  10.1 48.3 all-gather.4
  60.4 88.5 all-gather.6
  357.2 42.7 reduce-scatter.1
where the time goes:
time: 409 us; the launch traced here: 408 us
  waiting for transfers between devices  238 us (58%)
  matrix products  92.1 us (23%)
  local copies, waits for them, and re-layouts  29.9 us (7%)
  other arithmetic  19.5 us (5%)
  between operations  13.9 us (3%)
  blocking collectives  9.03 us (2%)
  starting transfers between devices  5.41 us (1%)
    all_to_all x1, waiting for transfers between devices, body(): lax.all_to_all(partial_value.reshape(expert_devices, local_experts * capa...  94.6 us
    all_gather x1, waiting for transfers between devices, body(): both = lax.all_gather(both, 'expert', axis=1, tiled=False)  75.3 us
    all_gather x1, waiting for transfers between devices, body(): lax.all_gather(jnp.stack([tokens, grad_out]), 'edata', axis=2, tiled=True)  49.4 us
    reduce_scatter x1, waiting for transfers between devices, body(): lax.psum_scatter(per_token, 'edata', scatter_dimension=1, tiled=True)  19 us
    dot_general x1, matrix products, body(): jnp.einsum('sxcf,xfd->sxcd', up_grad, w_up, preferred_element_type=jnp.fl...  13 us
    slice x1, local copies, waits for them, and re-layouts, body(): all_x, all_dy = (both[0], both[1])  9.49 us
    convert_element_type x1, local copies, waits for them, and re-layouts, body(): partial_value = partial_value.astype(jnp.bfloat16)  9.44 us
    dot_general x1, matrix products, body(): jnp.einsum('sxcd,xfd->sxcf', slot_dy, w_down, preferred_element_type=jnp....  9.36 us
  transfers between devices with their start and end apart: 4, of which 4 were waited for; matrix products, arithmetic and copies ran while one was open for 13% of the time, Pallas kernels for 0%

commit v1 on v0

--- a/solution.py
+++ b/solution.py
@@ -34,7 +34,15 @@
     hit = hit.reshape(expert_devices, token_count, top_count, local_experts, capacity)
     pick = jnp.sum(hit.astype(jnp.int32), 2).astype(jnp.bfloat16)
     prob_of = jnp.sum(jnp.where(hit, all_prob[:, :, :, None, None], 0.0), (1, 2))
-    both = lax.all_gather(jnp.stack([tokens, grad_out]), "edata", axis=2, tiled=True)
+    shard = jnp.stack([tokens, grad_out])
+    ways, here = (lax.axis_size("edata"), lax.axis_index("edata"))
+    both, reach = (shard, 1)
+    while reach < ways:
+        theirs = lax.ppermute(both, "edata", [(d, d ^ reach) for d in range(ways)])
+        mine_first = jnp.concatenate([both, theirs], axis=2)
+        theirs_first = jnp.concatenate([theirs, both], axis=2)
+        both = jnp.where(here & reach == 0, mine_first, theirs_first)
+        reach = 2 * reach
     both = lax.all_gather(both, "expert", axis=1, tiled=False)
     all_x, all_dy = (both[0], both[1])
     slot_x = jnp.einsum("stxc,std->sxcd", pick, all_x, preferred_element_type=jnp.float32).astype(

time: 409 us -> 421 us (1.029)
  local copies, waits for them, and re-layouts: 29.9 us -> 20.4 us
  waiting for transfers between devices: 238 us -> 246 us
  starting transfers between devices: 5.41 us -> 11.4 us
  matrix products: 92.1 us -> 97.1 us
    ppermute x0 -> x2, waiting for transfers between devices: none -> 55.3 us  [body(): theirs = lax.ppermute(both, 'edata', [(d, d ^ reach) for d in range(ways)])]
    all_gather x1 -> x0, waiting for transfers between devices: 49.4 us -> none  [body(): lax.all_gather(jnp.stack([tokens, grad_out]), 'edata', axis=2, tiled=True)]
    slice x1 -> x0, local copies, waits for them, and re-layouts: 9.49 us -> none  [body(): all_x, all_dy = (both[0], both[1])]
    ppermute x0 -> x2, starting transfers between devices: none -> 5.94 us  [body(): theirs = lax.ppermute(both, 'edata', [(d, d ^ reach) for d in range(ways)])]
    dot_general x1, matrix products: 5.46 us -> 10.2 us  [body(): jnp.einsum('stxc,std->sxcd', pick, all_x, preferred_element_type=jnp.floa...]
  transfers between devices with their start and end apart: 4 -> 5, of which waited for: 4 -> 5; matrix products, arithmetic and copies ran while one was open for 13% -> 12% of each run, Pallas kernels for 0% -> 0%
where the time goes in v1:
time: 421 us
  waiting for transfers between devices  246 us (58%)
  matrix products  97.1 us (23%)
  other arithmetic  22.7 us (5%)
  local copies, waits for them, and re-layouts  20.4 us (5%)
  between operations  14.2 us (3%)
  starting transfers between devices  11.4 us (3%)
  blocking collectives  8.98 us (2%)
    all_to_all x1, waiting for transfers between devices, body(): lax.all_to_all(partial_value.reshape(expert_devices, local_experts * capa...  94.4 us
    all_gather x1, waiting for transfers between devices, body(): both = lax.all_gather(both, 'expert', axis=1, tiled=False)  77.2 us
    ppermute x2, waiting for transfers between devices, body(): theirs = lax.ppermute(both, 'edata', [(d, d ^ reach) for d in range(ways)])  55.3 us
    reduce_scatter x1, waiting for transfers between devices, body(): lax.psum_scatter(per_token, 'edata', scatter_dimension=1, tiled=True)  19 us
    dot_general x1, matrix products, body(): jnp.einsum('sxcf,xfd->sxcd', up_grad, w_up, preferred_element_type=jnp.fl...  13 us
    dot_general x1, matrix products, body(): jnp.einsum('stxc,std->sxcd', pick, all_x, preferred_element_type=jnp.floa...  10.2 us
    convert_element_type x1, local copies, waits for them, and re-layouts, body(): partial_value = partial_value.astype(jnp.bfloat16)  9.45 us
    dot_general x1, matrix products, body(): jnp.einsum('sxcd,xfd->sxcf', slot_dy, w_down, preferred_element_type=jnp....  9.36 us
  transfers between devices with their start and end apart: 5, of which 5 were waited for; matrix products, arithmetic and copies ran while one was open for 12% of the time, Pallas kernels for 0%

profile of v1, /device:TPU:0, one launch (start us, length us, event | category | flops | bytes accessed | tf_op | source)
XLA Modules:
  0.0 420.7 jit_solution(1484195299818669656)
XLA Ops:
  8.3 3.1 collective-permute-start
  11.4 11.9 %collective-permute-done = bf16[2,128,1024]{2,1,0:T(8,128)(2,1)S(1)} collective-permute-done((bf16[2,128,1024]{2,1,0:T(8,128)(2,1)S(1)}, bf16[2,128,1024]{2,1,0:T(8,128)(2,1)S(1)}, u32[]{:S(2)}, u32[]{:S(2)}) %collective-permute-start) | collective-permute-done | bytes 524320 | tf_op jit(solution)/shard_map/ppermute | solution.py:41
  24.9 2.8 collective-permute-start.1
  29.3 43.3 %collective-permute-done.1 = bf16[2,128,2048]{2,1,0:T(8,128)(2,1)S(1)} collective-permute-done((bf16[2,128,2048]{2,1,0:T(8,128)(2,1)S(1)}, bf16[2,128,2048]{2,1,0:T(8,128)(2,1)S(1)}, u32[]{:S(2)}, u32[]{:S(2)}) %collective-permute-start.1) | collective-permute-done | bytes 1048608 | tf_op jit(solution)/shard_map/ppermute | solution.py:41
  74.9 9.0 %all-gather = f32[2,1024,8]{1,2,0:T(8,128)S(1)} all-gather(f32[2,128,8]{1,2,0:T(8,128)S(1)} %pad_maximum_fusion.1), channel_id=2, replica_groups=mesh['edata'=4,'expert'=8] {'expert'}, dimensions={1}, use_global_device_ids=true | all-gather | bytes 73728 | tf_op jit(solution)/shard_map/all_gather | solution.py:28
  88.5 77.2 %all-gather.3.cloned.1.call-done = bf16[2,8,128,4096]{3,2,1,0:T(8,128)(2,1)} async-done(((bf16[2,1,128,4096]{3,2,1,0:T(8,128)(2,1)}), bf16[2,8,128,4096]{3,2,1,0:T(8,128)(2,1)}) %all-gather.3.cloned.1.call-update) | async-done | bytes 16777232 | tf_op jit(solution)/shard_map/all_gather | solution.py:46
  165.7 10.2 %fusion.7 = bf16[8,2,80,4096]{3,2,1,0:T(8,128)(2,1)} fusion(bf16[2,8,128,4096]{3,2,1,0:T(8,128)(2,1)} %all-gather.3.cloned.1.call-done, s32[8,128,2,80]{1,3,2,0:T(8,128)S(1)} %convert_reduce_fusion), kind=kOutput, calls=%fused_computation.15 | convolution fusion | flops 1347584000 | bytes 19529728 | tf_op jit(solution)/shard_map/stxc,std->sxcd/dot_general | solution.py:48
  175.9 9.3 %fusion.38 = f32[8,2,80,256]{3,2,0,1:T(8,128)} fusion(bf16[2,256,4096]{2,1,0:T(8,128)(2,1)} %param.11, bf16[8,2,80,4096]{3,2,1,0:T(8,128)(2,1)} %fusion.7), kind=kOutput, calls=%fused_computation.40 | convolution fusion | flops 2684354560 | bytes 15990784 | tf_op jit(solution)/shard_map/sxcd,xfd->sxcf/dot_general | solution.py:53
  185.2 6.3 %fusion.33 = f32[8,2,80,256]{3,2,0,1:T(8,128)} fusion(bf16[2,256,4096]{2,1,0:T(8,128)(2,1)} %param.12, bf16[8,2,80,4096]{3,2,1,0:T(8,128)(2,1)S(1)} %copy-done), kind=kOutput, calls=%fused_computation.39 | convolution fusion | flops 2684354560 | bytes 15990784 | tf_op jit(solution)/shard_map/sxcd,xfd->sxcf/dot_general | solution.py:54
  191.6 8.8 %multiply_convert_fusion = bf16[8,2,80,4096]{3,2,1,0:T(8,128)(2,1)} fusion(f32[8,2,80]{2,1,0:T(2,128)S(1)} %select_reduce_fusion, bf16[2,8,128,4096]{3,2,1,0:T(8,128)(2,1)} %all-gather.3.cloned.1.call-done, s32[8,128,2,80]{1,3,2,0:T(8,128)S(1)} %convert_reduce_fusion), kind=kOutput, calls=%fused_computation.1 | convolution fusion | flops 1352826880 | bytes 19534848 | tf_op jit(solution)/shard_map/stxc,std->sxcd/dot_general | solution.py:51
  200.3 9.4 %multiply_convert_fusion.2 = (bf16[8,2,80,256]{3,2,0,1:T(8,128)(2,1)S(1)}, bf16[8,2,80,256]{3,2,0,1:T(8,128)(2,1)S(1)}) fusion(f32[8,2,80,256]{3,2,0,1:T(8,128)} %fusion.38, f32[8,2,80,256]{3,2,0,1:T(8,128)} %fusion.33, bf16[2,256,4096]{2,1,0:T(8,128)(2,1)} %param.13, bf16[8,2,80,4096]{3,2,1,0:T(8,128)(2,1)} %multiply_convert_fusion), kind=kOutput, calls=%fused_computation.43 | convolution fusion | flops 2688614400 | bytes 18612224 | tf_op jit(solution)/shard_map/sxcd,xfd->sxcf/dot_general | solution.py:58
  209.7 8.5 %fusion.23 = f32[2,8,80,4096]{3,2,1,0:T(8,128)} fusion(bf16[8,2,80,256]{3,2,0,1:T(8,128)(2,1)S(1)} %get-tuple-element.5, bf16[2,256,4096]{2,1,0:T(8,128)(2,1)S(1)} %copy-done.1), kind=kOutput, calls=%fused_computation.28 | convolution fusion | flops 2684354560 | bytes 25821184 | tf_op jit(solution)/shard_map/sxcf,xfd->sxcd/dot_general | solution.py:70
  218.2 13.0 %fusion = bf16[8,2,80,4096]{3,2,0,1:T(8,128)(2,1)} fusion(f32[2,8,80,4096]{3,2,1,0:T(8,128)} %fusion.23, bf16[8,2,80,256]{3,2,0,1:T(8,128)(2,1)S(1)} %get-tuple-element.4, bf16[2,256,4096]{2,1,0:T(8,128)(2,1)} %param.12), kind=kOutput, calls=%fused_computation.2 | convolution fusion | flops 2694840320 | bytes 36306944 | tf_op jit(solution)/shard_map/sxcf,xfd->sxcd/dot_general | solution.py:73
  231.2 9.4 %copy.42 = bf16[8,2,80,4096]{3,2,1,0:T(8,128)(2,1)} copy(bf16[8,2,80,4096]{3,2,0,1:T(8,128)(2,1)} %fusion) | data formatting | bytes 20971520 | tf_op jit(solution)/shard_map/convert_element_type | solution.py:76
  240.6 5.2 %all-to-all-start = ((bf16[8,160,4096]{2,1,0:T(8,128)(2,1)}), bf16[8,160,4096]{2,1,0:T(8,128)(2,1)}, u32[]{:S(2)}, u32[]{:S(2)}) async-start(bf16[8,160,4096]{2,1,0:T(8,128)(2,1)} %bitcast.90), calls=%async_computation | async-start | bytes 20971520 | tf_op jit(solution)/shard_map/all_to_all | solution.py:77
  247.3 7.9 %and_convert_fusion = s32[1024,16,80]{2,1,0:T(8,128)} fusion(pred[1024,80]{1,0:T(8,128)(4,1)S(1)} %iota_compare_fusion.9, pred[1024,16]{1,0:T(8,128)(4,1)S(1)} %copy.35), kind=kLoop, calls=%fused_computation.14 | loop fusion | flops 2621440 | bytes 5341184 | tf_op jit(solution)/shard_map/convert_element_type | solution.py:89
  255.1 9.1 %reshape.193 = s32[128,8,1280]{2,1,0:T(8,128)} reshape(s32[1024,16,80]{2,1,0:T(8,128)} %and_convert_fusion) | data formatting | bytes 10485760 | tf_op jit(solution)/shard_map/convert_element_type | solution.py:89
  264.2 3.7 reduce_sum.37
  268.0 94.4 %all-to-all-done = bf16[8,160,4096]{2,1,0:T(8,128)(2,1)} async-done(((bf16[8,160,4096]{2,1,0:T(8,128)(2,1)}), bf16[8,160,4096]{2,1,0:T(8,128)(2,1)}, u32[]{:S(2)}, u32[]{:S(2)}) %all-to-all-start) | async-done | bytes 10485792 | tf_op jit(solution)/shard_map/all_to_all | solution.py:77
  362.3 6.9 %fusion.58 = f32[128,4096]{1,0:T(8,128)} fusion(bf16[1280,4096]{1,0:T(8,128)(2,1)} %bitcast.28, s32[128,1280]{1,0:T(8,128)S(1)} %reduce_sum.37), kind=kOutput, calls=%fused_computation.55 | convolution fusion | flops 1342341120 | bytes 13238272 | tf_op jit(solution)/shard_map/tq,qd->td/dot_general | solution.py:91
  369.2 9.2 %bitcast_convert_fusion.1 = bf16[2,256,4096]{2,1,0:T(8,128)(2,1)} fusion(bf16[8,2,80,256]{3,2,0,1:T(8,128)(2,1)S(1)} %get-tuple-element.4, bf16[8,2,80,4096]{3,2,1,0:T(8,128)(2,1)} %fusion.7), kind=kOutput, calls=%fused_computation.12 | convolution fusion | flops 2686451712 | bytes 15335424 | tf_op jit(solution)/shard_map/sxcf,sxcd->xfd/dot_general | solution.py:64
  378.4 9.3 %bitcast_convert_fusion.2 = bf16[2,256,4096]{2,1,0:T(8,128)(2,1)} fusion(bf16[8,2,80,256]{3,2,0,1:T(8,128)(2,1)S(1)} %get-tuple-element.5, bf16[8,2,80,4096]{3,2,1,0:T(8,128)(2,1)} %fusion.7), kind=kOutput, calls=%fused_computation.13 | convolution fusion | flops 2686451712 | bytes 15335424 | tf_op jit(solution)/shard_map/sxcf,sxcd->xfd/dot_general | solution.py:61
  387.7 5.3 %bitcast_convert_fusion = bf16[2,256,4096]{2,1,0:T(8,128)(2,1)} fusion(bf16[8,2,80,4096]{3,2,1,0:T(8,128)(2,1)S(1)} %bitcast.92, f32[8,2,80,256]{3,2,0,1:T(8,128)S(1)} %copy-done.5, f32[8,2,80,256]{3,2,0,1:T(8,128)S(1)} %copy-done.4), kind=kOutput, calls=%fused_computation.11 | convolution fusion | flops 2688417792 | bytes 17301504 | tf_op jit(solution)/shard_map/sxcf,sxcd->xfd/dot_general | solution.py:67
  393.1 19.0 %reduce-scatter.2.cloned.1.call-done = f32[128,1024]{1,0:T(8,128)} async-done(((f32[128,4096]{1,0:T(8,128)}), f32[128,1024]{1,0:T(8,128)}) %reduce-scatter.2.cloned.1.call-update) | async-done | bytes 524304 | tf_op jit(solution)/shard_map/reduce_scatter | solution.py:97
  (47 shorter events, 14.3 us)
Async XLA Ops:
  7.2 158.6 %all-gather.3.cloned.1.call-start = ((), (), s32[]{:S(2)}) async-start(), calls=%async_computation.2 | async-start | bytes 18874368 | tf_op jit(solution)/shard_map/all_gather | solution.py:46
  8.3 15.0 %collective-permute-start = (bf16[2,128,1024]{2,1,0:T(8,128)(2,1)S(1)}, bf16[2,128,1024]{2,1,0:T(8,128)(2,1)S(1)}, u32[]{:S(2)}, u32[]{:S(2)}) collective-permute-start(bf16[2,128,1024]{2,1,0:T(8,128)(2,1)S(1)} %pad_maximum_fusion), channel_id=1, source_target_pairs={{0,8},{8,0},{16,24},{24,16},{1,9},{9,1},{17,25},{25,17},{2,10},{10... | collective-permute-start | bytes 1572872 | tf_op jit(solution)/shard_map/ppermute | solution.py:41
  24.9 47.8 %collective-permute-start.1 = (bf16[2,128,2048]{2,1,0:T(8,128)(2,1)S(1)}, bf16[2,128,2048]{2,1,0:T(8,128)(2,1)S(1)}, u32[]{:S(2)}, u32[]{:S(2)}) collective-permute-start(bf16[2,128,2048]{2,1,0:T(8,128)(2,1)S(1)} %maximum_select_fusion.1), channel_id=1, source_target_pairs={{0,16},{8,24},{16,0},{24,8},{1,17},{9,25},{17,1},{25,9},{2,18},{10... | collective-permute-start | bytes 3145736 | tf_op jit(solution)/shard_map/ppermute | solution.py:41
  27.7 47.1 %copy-start.2 = (s32[128,8]{0,1:T(8,128)S(1)}, s32[128,8]{0,1:T(8,128)}, u32[]{:S(2)}) copy-start(s32[128,8]{0,1:T(8,128)} %param.9) | copy-start | bytes 12292
  27.7 47.1 %copy-start.3 = (f32[128,8]{0,1:T(8,128)S(1)}, f32[128,8]{0,1:T(8,128)}, u32[]{:S(2)}) copy-start(f32[128,8]{0,1:T(8,128)} %param.10) | copy-start | bytes 12292
  175.9 9.3 %copy-start = (bf16[8,2,80,4096]{3,2,1,0:T(8,128)(2,1)S(1)}, bf16[8,2,80,4096]{3,2,1,0:T(8,128)(2,1)}, u32[]{:S(2)}) copy-start(bf16[8,2,80,4096]{3,2,1,0:T(8,128)(2,1)} %fusion.7) | copy-start | bytes 31457284
  200.3 9.4 %copy-start.1 = (bf16[2,256,4096]{2,1,0:T(8,128)(2,1)S(1)}, bf16[2,256,4096]{2,1,0:T(8,128)(2,1)}, u32[]{:S(2)}) copy-start(bf16[2,256,4096]{2,1,0:T(8,128)(2,1)} %param.11) | copy-start | bytes 12582916
  240.6 121.7 %all-to-all-start = ((bf16[8,160,4096]{2,1,0:T(8,128)(2,1)}), bf16[8,160,4096]{2,1,0:T(8,128)(2,1)}, u32[]{:S(2)}, u32[]{:S(2)}) async-start(bf16[8,160,4096]{2,1,0:T(8,128)(2,1)} %bitcast.90), calls=%async_computation | async-start | bytes 20971520 | tf_op jit(solution)/shard_map/all_to_all | solution.py:77
  245.8 166.3 %reduce-scatter.2.cloned.1.call-start = ((), (), s32[]{:S(2)}) async-start(), calls=%async_computation.3 | async-start | bytes 2621440 | tf_op jit(solution)/shard_map/reduce_scatter | solution.py:97
  369.2 18.5 %slice-start = ((s8[10485760]{0:T(1024)(128)(4,1)}), s8[4194304]{0:T(1024)(128)(4,1)S(1)}, s32[]{:S(2)}) async-start(s8[10485760]{0:T(1024)(128)(4,1)} %bitcast.91), calls=%async_computation.4 | async-start | bytes 8388608
  369.2 18.5 %slice-start.1 = ((s8[10485760]{0:T(1024)(128)(4,1)}), s8[4194304]{0:T(1024)(128)(4,1)S(1)}, s32[]{:S(2)}) async-start(s8[10485760]{0:T(1024)(128)(4,1)} %bitcast.91), calls=%async_computation.5 | async-start | bytes 8388608
  378.4 9.3 %slice-start.2 = ((s8[10485760]{0:T(1024)(128)(4,1)}), s8[2097152]{0:T(1024)(128)(4,1)S(1)}, s32[]{:S(2)}) async-start(s8[10485760]{0:T(1024)(128)(4,1)} %bitcast.91), calls=%async_computation.6 | async-start | bytes 4194304
  378.4 9.3 %copy-start.4 = (f32[8,2,80,256]{3,2,0,1:T(8,128)S(1)}, f32[8,2,80,256]{3,2,0,1:T(8,128)}, u32[]{:S(2)}) copy-start(f32[8,2,80,256]{3,2,0,1:T(8,128)} %fusion.38) | copy-start | bytes 3932164
  378.4 9.3 %copy-start.5 = (f32[8,2,80,256]{3,2,0,1:T(8,128)S(1)}, f32[8,2,80,256]{3,2,0,1:T(8,128)}, u32[]{:S(2)}) copy-start(f32[8,2,80,256]{3,2,0,1:T(8,128)} %fusion.33) | copy-start | bytes 3932164
Sparse Core Ops, SparseCore 0:
  74.9 90.7 all-gather.2
  369.3 42.7 reduce-scatter.1
